TPU v7x, 32 devices: a whole 2x2x4 slice. The times are simulated.
32 devices in a mesh: tm: 16 (over z, x, core), rows: 2 (over y).
Axes of the slice: x: 2, y: 2, z: 4, core: 2. Of those that a mesh axis runs over, the one named last changes fastest.
Arguments:
- video: bfloat16 [32, 16, 480, 128], P('tm', 'rows'), may hold values from -1000 to 1000, as said below
- spatial_weight: bfloat16 [3, 3, 128, 128], replicated, may hold values from -0.1875 to 0.1875
- norm_gain: float32 [128], replicated, may hold values from 0.5 to 1.5
- norm_shift: float32 [128], replicated, may hold values from -3 to 3
- temporal_weight: bfloat16 [3, 3, 128, 128], replicated, may hold values from -0.3125 to 0.3125
Outputs:
- encoded: bfloat16 [32, 16, 480, 128], P('tm', 'rows')
Inputs may be any that keep to these rules, and one draw needn't show every extreme that they name: `video`: feature values are finite and of moderate size.
All inputs are finite; a program needn't handle non-finite values.
Results may differ from a plain program's by a relative error of at most 0.0065.
Values may be sent and summed in bfloat16 or wider, within the bound.
No kernel may reach another device: no remote copies, remote signals or barrier semaphores. Data moves between devices by JAX's collectives and lax.ppermute only.
A program may use at most 64 MiB of HBM per device.

v0:
```python
import jax
import jax.numpy as jnp
from jax import lax
from jax.sharding import PartitionSpec as P

GROUPS = 32


def padded_2(array, sides, width):
    for axis, dim in sides:
        size, length = (lax.axis_size(axis), array.shape[dim])
        up = [(i, (i + 1) % size) for i in range(size - 1)]
        down = [(j, i) for i, j in up]
        last = lax.slice_in_dim(array, length - width, length, axis=dim)
        leading = lax.slice_in_dim(array, 0, width, axis=dim)
        before = lax.ppermute(last, axis, up)
        after = lax.ppermute(leading, axis, down)
        array = jnp.concatenate([before, array, after], axis=dim)
    return array


def temporal_layer(extended, lead, dilation, kernels):
    own = extended.shape[0] - lead
    total = extended[lead:].astype(jnp.float32)
    for tap_index in range(3):
        start = lead - tap_index * dilation
        total = total + jnp.einsum(
            "trwc,cd->trwd",
            extended[start : start + own],
            kernels[tap_index],
            preferred_element_type=jnp.float32,
        )
    return total.astype(jnp.bfloat16)


def body(video, spatial_weight, norm_gain, norm_shift, temporal_weight):
    fr_local, band, width, chans = video.shape
    padded = padded_2(video, (("rows", 1),), 1)
    padded = jnp.pad(padded, ((0, 0), (0, 0), (1, 1), (0, 0)))
    pieces = [
        padded[:, row_tap : row_tap + band, col_tap : col_tap + width, :]
        for row_tap in range(3)
        for col_tap in range(3)
    ]
    patches = jnp.concatenate(pieces, axis=-1).reshape(fr_local * band * width, 9 * chans)
    conv = jnp.dot(
        patches, spatial_weight.reshape(9 * chans, chans), preferred_element_type=jnp.float32
    )
    per_group = chans // GROUPS
    grouped = conv.reshape(fr_local, band, width, GROUPS, per_group)
    part_sum = jnp.sum(grouped, axis=(1, 2, 4))
    part_square = jnp.sum(grouped * grouped, axis=(1, 2, 4))
    total_sum, total_square = lax.psum((part_sum, part_square), "rows")
    count = jnp.float32(band * lax.axis_size("rows") * width * per_group)
    mean = total_sum / count
    var = total_square / count - mean * mean
    normed = (grouped - mean[:, None, None, :, None]) * lax.rsqrt(var + 1e-05)[
        :, None, None, :, None
    ]
    normed = normed.reshape(fr_local, band, width, chans) * norm_gain + norm_shift
    hidden = jax.nn.silu(normed).astype(jnp.bfloat16)
    current = lax.all_to_all(hidden, "tm", split_axis=2, concat_axis=0, tiled=True)
    for layer, dilation in enumerate((1, 2, 4)):
        lead = 2 * dilation
        extended = jnp.pad(current, ((lead, 0), (0, 0), (0, 0), (0, 0)))
        current = temporal_layer(extended, lead, dilation, temporal_weight[layer])
    return lax.all_to_all(current, "tm", split_axis=0, concat_axis=2, tiled=True)


def solution(mesh):
    return jax.shard_map(
        body,
        mesh=mesh,
        in_specs=(P("tm", "rows", None, None), P(), P(), P(), P()),
        out_specs=P("tm", "rows", None, None),
        check_vma=False,
    )
```

profile of v0, /device:TPU:1, one launch (start us, length us, event | category | flops | bytes accessed | tf_op | source)
XLA Modules:
  0.0 154.6 jit_solution(4578269416225532073)
XLA Ops:
  0.0 1.1 fusion.36
  1.1 4.0 %collective-permute-start = (bf16[2,1,480,128]{3,2,1,0:T(8,128)(2,1)S(1)}, bf16[2,1,480,128]{3,2,1,0:T(8,128)(2,1)S(1)}, u32[]{:S(2)}, u32[]{:S(2)}) collective-permute-start(bf16[2,1,480,128]{3,2,1,0:T(8,128)(2,1)S(1)} %get-tuple-element.9), channel_id=1, source_target_pairs={{0,1},{2,3},{4,5},{6,7},{8,9},{10,11},{12,13},{14,15},{16,17},{18,... | collective-permute-start | bytes 737288 | tf_op jit(solution)/shard_map/ppermute | solution.py:16
  5.1 1.3 collective-permute-start.1
  6.4 1.2 copy.14
  7.6 0.1 dot_general.35
  7.6 0.0 copy-start
  7.7 2.0 %collective-permute-done = bf16[2,1,480,128]{3,2,1,0:T(8,128)(2,1)S(1)} collective-permute-done((bf16[2,1,480,128]{3,2,1,0:T(8,128)(2,1)S(1)}, bf16[2,1,480,128]{3,2,1,0:T(8,128)(2,1)S(1)}, u32[]{:S(2)}, u32[]{:S(2)}) %collective-permute-start) | collective-permute-done | bytes 245792 | tf_op jit(solution)/shard_map/ppermute | solution.py:16
  9.7 3.8 %collective-permute-done.1 = bf16[2,1,480,128]{3,2,1,0:T(8,128)(2,1)S(1)} collective-permute-done((bf16[2,1,480,128]{3,2,1,0:T(8,128)(2,1)S(1)}, bf16[2,1,480,128]{3,2,1,0:T(8,128)(2,1)S(1)}, u32[]{:S(2)}, u32[]{:S(2)}) %collective-permute-start.1) | collective-permute-done | bytes 245792 | tf_op jit(solution)/shard_map/ppermute | solution.py:17
  13.5 2.1 %fusion.7 = bf16[2,10,482,128]{3,2,1,0:T(8,128)(2,1)S(1)} fusion(bf16[2,1,480,128]{3,2,1,0:T(8,128)(2,1)S(1)} %collective-permute-done.1, bf16[2,8,480,128]{3,2,1,0:T(8,128)(2,1)} %param.5, bf16[2,1,480,128]{3,2,1,0:T(8,128)(2,1)S(1)} %collective-permute-done), kind=kLoop, calls=%fused_computation.15 | loop fusion | flops 14807040 | bytes 4925440 | tf_op jit(solution)/shard_map/concatenate | solution.py:18
  15.6 0.3 slice_dynamic-update-slice_fusion.5
  15.9 0.0 copy-done
  15.9 0.5 fusion.9
  16.4 0.8 slice_dynamic-update-slice_fusion.4
  17.2 0.5 slice_dynamic-update-slice_fusion.3
  17.7 0.5 constant_dynamic-update-slice_fusion
  18.2 0.8 slice_dynamic-update-slice_fusion.2
  19.0 0.5 slice_dynamic-update-slice_fusion.1
  19.5 0.5 fusion.8
  20.0 0.8 slice_dynamic-update-slice_fusion
  20.8 7.1 %fusion.35 = (f32[2,32]{1,0:T(2,128)S(1)}, f32[2,32]{1,0:T(2,128)S(1)}, f32[2,8,480,32,4]{2,3,4,1,0:T(8,128)}) fusion(bf16[32,4,1152,1,1]{2,1,0,4,3:T(4,128)(2,1)S(1)} %bitcast.100, bf16[2,8,480,1152]{3,2,1,0:T(8,128)(2,1)S(1)} %slice_dynamic-update-slice_fusion), kind=kOutput, calls=%fused_computation.54 | convolution fusion | flops 2267873280 | bytes 21922304 | tf_op jit(solution)/shard_map/dot_general | solution.py:46
  27.9 3.9 %all-reduce.4 = (f32[2,32]{1,0:T(2,128)S(1)}, f32[2,32]{1,0:T(2,128)S(1)}) all-reduce(f32[2,32]{1,0:T(2,128)S(1)} %get-tuple-element.6, f32[2,32]{1,0:T(2,128)S(1)} %get-tuple-element.5), channel_id=1, replica_groups=mesh['tm'=16,'rows'=2] {'rows'}, use_global_device_ids=true, to_apply=%region_3.4 | all-reduce | flops 128 | bytes 1024 | tf_op jit(solution)/shard_map/psum | solution.py:53
  31.8 2.9 %subtract_multiply_fusion = f32[2,8,480,32,4]{2,3,4,1,0:T(8,128)S(1)} fusion(f32[2,8,480,32,4]{2,3,4,1,0:T(8,128)} %get-tuple-element.13, f32[2,32]{1,0:T(2,128)S(1)} %get-tuple-element.12, f32[2,32]{1,0:T(2,128)S(1)} %get-tuple-element.11), kind=kLoop, calls=%fused_computation.7 | loop fusion | flops 1966080 | bytes 7864832 | tf_op jit(solution)/shard_map/mul | solution.py:57
  34.7 0.0 copy-start.2
  34.7 0.0 copy-start.3
  34.7 2.4 %copy.16 = f32[2,8,480,32,4]{2,1,4,3,0:T(8,128)S(1)} copy(f32[2,8,480,32,4]{2,3,4,1,0:T(8,128)S(1)} %subtract_multiply_fusion) | data formatting | bytes 7864320 | tf_op jit(solution)/shard_map/mul | solution.py:57
  37.2 0.0 copy-done.2
  37.2 0.0 copy-done.3
  37.2 1.4 multiply_convert_fusion
  38.7 3.4 %copy.17 = bf16[2,8,480,128]{3,1,0,2:T(8,128)(2,1)} copy(bf16[2,8,480,128]{2,1,3,0:T(8,128)(2,1)S(1)} %multiply_convert_fusion) | data formatting | bytes 3932160 | tf_op jit(solution)/shard_map/convert_element_type | solution.py:61
  42.0 0.0 copy-start.1
  42.0 54.3 %all_to_all.36 = bf16[2,8,480,128]{3,1,0,2:T(8,128)(2,1)S(1)} all-to-all(bf16[2,8,480,128]{3,1,0,2:T(8,128)(2,1)} %copy.17), channel_id=1, replica_groups=mesh['tm'=16,'rows'=2] {'tm'}, dimensions={2} | all-to-all | bytes 3932160 | tf_op jit(solution)/shard_map/all_to_all | solution.py:62
  96.4 0.3 copy.19
  96.7 0.0 copy-done.1
  96.7 0.7 fusion.22
  97.4 0.7 fusion.24
  98.0 0.9 add_convert_fusion.2
  99.0 0.6 fusion.17
  99.6 0.7 fusion.19
  100.3 1.0 add_convert_fusion.1
  101.3 0.7 fusion.12
  102.0 0.7 fusion.14
  102.6 1.0 add_convert_fusion
  103.6 49.4 %all_to_all.37 = bf16[32,8,30,128]{3,1,2,0:T(8,128)(2,1)S(1)} all-to-all(bf16[32,8,30,128]{3,1,2,0:T(8,128)(2,1)S(1)} %add_convert_fusion), channel_id=1, replica_groups=mesh['tm'=16,'rows'=2] {'tm'}, dimensions={0} | all-to-all | bytes 3932160 | tf_op jit(solution)/shard_map/all_to_all | solution.py:67
  153.0 0.1 copy.20
  153.1 1.5 copy.21
  (1 shorter events, 0.0 us)
Async XLA Ops:
  1.1 8.6 %collective-permute-start = (bf16[2,1,480,128]{3,2,1,0:T(8,128)(2,1)S(1)}, bf16[2,1,480,128]{3,2,1,0:T(8,128)(2,1)S(1)}, u32[]{:S(2)}, u32[]{:S(2)}) collective-permute-start(bf16[2,1,480,128]{3,2,1,0:T(8,128)(2,1)S(1)} %get-tuple-element.9), channel_id=1, source_target_pairs={{0,1},{2,3},{4,5},{6,7},{8,9},{10,11},{12,13},{14,15},{16,17},{18,... | collective-permute-start | bytes 737288 | tf_op jit(solution)/shard_map/ppermute | solution.py:16
  5.1 8.4 %collective-permute-start.1 = (bf16[2,1,480,128]{3,2,1,0:T(8,128)(2,1)S(1)}, bf16[2,1,480,128]{3,2,1,0:T(8,128)(2,1)S(1)}, u32[]{:S(2)}, u32[]{:S(2)}) collective-permute-start(bf16[2,1,480,128]{3,2,1,0:T(8,128)(2,1)S(1)} %get-tuple-element.10), channel_id=1, source_target_pairs={{1,0},{3,2},{5,4},{7,6},{9,8},{11,10},{13,12},{15,14},{17,16},{19,... | collective-permute-start | bytes 737288 | tf_op jit(solution)/shard_map/ppermute | solution.py:17
  7.6 8.3 %copy-start = (bf16[2,8,480,128]{3,2,1,0:T(8,128)(2,1)S(1)}, bf16[2,8,480,128]{3,2,1,0:T(8,128)(2,1)}, u32[]{:S(2)}) copy-start(bf16[2,8,480,128]{3,2,1,0:T(8,128)(2,1)} %param.5) | copy-start | bytes 5898244
  34.7 2.5 %copy-start.2 = (f32[128]{0:T(128)S(1)}, f32[128]{0:T(128)}, u32[]{:S(2)}) copy-start(f32[128]{0:T(128)} %param.8) | copy-start | bytes 1540
  34.7 2.5 %copy-start.3 = (f32[128]{0:T(128)S(1)}, f32[128]{0:T(128)}, u32[]{:S(2)}) copy-start(f32[128]{0:T(128)} %param.7) | copy-start | bytes 1540
  42.0 54.7 %copy-start.1 = (bf16[3,3,128,128]{3,2,1,0:T(8,128)(2,1)S(1)}, bf16[3,3,128,128]{3,2,1,0:T(8,128)(2,1)}, u32[]{:S(2)}) copy-start(bf16[3,3,128,128]{3,2,1,0:T(8,128)(2,1)} %param.9) | copy-start | bytes 884740
where the time goes:
time: 155 us
  blocking collectives  108 us (70%)
  local copies, waits for them, and re-layouts  14.3 us (9%)
  matrix products  13.9 us (9%)
  other arithmetic  7.38 us (5%)
  waiting for transfers between devices  5.84 us (4%)
  starting transfers between devices  5.28 us (3%)
    all_to_all x1, blocking collectives, body(): lax.all_to_all(hidden, 'tm', split_axis=2, concat_axis=0, tiled=True)  54.3 us
    all_to_all x1, blocking collectives, body(): lax.all_to_all(current, 'tm', split_axis=0, concat_axis=2, tiled=True)  49.4 us
    dot_general x1, matrix products, body(): jnp.dot(patches, spatial_weight.reshape(9 * chans, chans), preferred_elem...  7.06 us
    dot_general x9, matrix products, temporal_layer(): jnp.einsum('trwc,cd->trwd', extended[start:start + own], kernels[tap_inde...  6.82 us
    ppermute x1, starting transfers between devices, padded_2(): before = lax.ppermute(last, axis, up)  3.99 us
    psum x1, blocking collectives, body(): total_sum, total_square = lax.psum((part_sum, part_square), 'rows')  3.95 us
    ppermute x1, waiting for transfers between devices, padded_2(): after = lax.ppermute(leading, axis, down)  3.81 us
    unnamed x14, local copies, waits for them, and re-layouts  3.41 us
  transfers between devices with their start and end apart: 2, of which 2 were waited for; matrix products, arithmetic and copies ran while one was open for 1% of the time, Pallas kernels for 0%

commit v1 on v0

--- a/solution.py
+++ b/solution.py
@@ -59,7 +59,10 @@
     ]
     normed = normed.reshape(fr_local, band, width, chans) * norm_gain + norm_shift
     hidden = jax.nn.silu(normed).astype(jnp.bfloat16)
-    current = lax.all_to_all(hidden, "tm", split_axis=2, concat_axis=0, tiled=True)
+    current = jnp.concatenate(
+        lax.all_to_all(jnp.stack(jnp.split(hidden, lax.axis_size("tm"), axis=2)), "tm", 0, 0),
+        axis=0,
+    )
     for layer, dilation in enumerate((1, 2, 4)):
         lead = 2 * dilation
         extended = jnp.pad(current, ((lead, 0), (0, 0), (0, 0), (0, 0)))

time: 155 us -> 191 us (1.23)
  local copies, waits for them, and re-layouts: 14.3 us -> 50.8 us
    another operation x0 -> x18, local copies, waits for them, and re-layouts: none -> 31.6 us  [body(): jnp.stack(jnp.split(hidden, lax.axis_size('tm'), axis=2))]
    unnamed x14 -> x39, local copies, waits for them, and re-layouts: 3.41 us -> 11.8 us
    convert_element_type x1 -> x0, local copies, waits for them, and re-layouts: 3.36 us -> none  [body(): hidden = jax.nn.silu(normed).astype(jnp.bfloat16)]
where the time goes in v1:
time: 191 us; the launch traced here: 190 us
  blocking collectives  107 us (56%)
  local copies, waits for them, and re-layouts  50.8 us (27%)
  matrix products  14 us (7%)
  other arithmetic  6.14 us (3%)
  waiting for transfers between devices  5.85 us (3%)
  starting transfers between devices  5.28 us (3%)
    all_to_all x1, blocking collectives, body(): lax.all_to_all(jnp.stack(jnp.split(hidden, lax.axis_size('tm'), axis=2)),...  54 us
    all_to_all x1, blocking collectives, body(): lax.all_to_all(current, 'tm', split_axis=0, concat_axis=2, tiled=True)  49.4 us
    another operation x18, local copies, waits for them, and re-layouts, body(): jnp.stack(jnp.split(hidden, lax.axis_size('tm'), axis=2))  31.6 us
    unnamed x39, local copies, waits for them, and re-layouts  11.8 us
    dot_general x1, matrix products, body(): jnp.dot(patches, spatial_weight.reshape(9 * chans, chans), preferred_elem...  7.07 us
    dot_general x9, matrix products, temporal_layer(): jnp.einsum('trwc,cd->trwd', extended[start:start + own], kernels[tap_inde...  6.92 us
    ppermute x1, starting transfers between devices, padded_2(): before = lax.ppermute(last, axis, up)  3.99 us
    psum x1, blocking collectives, body(): total_sum, total_square = lax.psum((part_sum, part_square), 'rows')  3.95 us
  transfers between devices with their start and end apart: 2, of which 2 were waited for; matrix products, arithmetic and copies ran while one was open for 1% of the time, Pallas kernels for 0%

profile of v1, /device:TPU:1, one launch (start us, length us, event | category | flops | bytes accessed | tf_op | source)
XLA Modules:
  0.0 189.8 jit_solution(1694492770635463129)
XLA Ops:
  0.0 1.2 fusion.36
  1.2 4.0 %collective-permute-start = (bf16[2,1,480,128]{3,2,1,0:T(8,128)(2,1)S(1)}, bf16[2,1,480,128]{3,2,1,0:T(8,128)(2,1)S(1)}, u32[]{:S(2)}, u32[]{:S(2)}) collective-permute-start(bf16[2,1,480,128]{3,2,1,0:T(8,128)(2,1)S(1)} %get-tuple-element.25), channel_id=1, source_target_pairs={{0,1},{2,3},{4,5},{6,7},{8,9},{10,11},{12,13},{14,15},{16,17},{18,... | collective-permute-start | bytes 737288 | tf_op jit(solution)/shard_map/ppermute | solution.py:16
  5.2 1.3 collective-permute-start.1
  6.5 1.2 copy.13
  7.7 0.1 dot_general.35
  7.8 2.0 %collective-permute-done = bf16[2,1,480,128]{3,2,1,0:T(8,128)(2,1)S(1)} collective-permute-done((bf16[2,1,480,128]{3,2,1,0:T(8,128)(2,1)S(1)}, bf16[2,1,480,128]{3,2,1,0:T(8,128)(2,1)S(1)}, u32[]{:S(2)}, u32[]{:S(2)}) %collective-permute-start) | collective-permute-done | bytes 245792 | tf_op jit(solution)/shard_map/ppermute | solution.py:16
  9.8 3.8 %collective-permute-done.1 = bf16[2,1,480,128]{3,2,1,0:T(8,128)(2,1)S(1)} collective-permute-done((bf16[2,1,480,128]{3,2,1,0:T(8,128)(2,1)S(1)}, bf16[2,1,480,128]{3,2,1,0:T(8,128)(2,1)S(1)}, u32[]{:S(2)}, u32[]{:S(2)}) %collective-permute-start.1) | collective-permute-done | bytes 245792 | tf_op jit(solution)/shard_map/ppermute | solution.py:17
  13.6 0.9 fusion.7
  14.5 0.3 slice_dynamic-update-slice_fusion.5
  14.9 0.5 fusion.9
  15.3 0.8 slice_dynamic-update-slice_fusion.4
  16.2 0.5 slice_dynamic-update-slice_fusion.3
  16.6 0.5 constant_dynamic-update-slice_fusion
  17.1 0.8 slice_dynamic-update-slice_fusion.2
  17.9 0.5 slice_dynamic-update-slice_fusion.1
  18.4 0.5 fusion.8
  18.9 0.8 slice_dynamic-update-slice_fusion
  19.7 7.1 %fusion.35 = (f32[2,32]{1,0:T(2,128)S(1)}, f32[2,32]{1,0:T(2,128)S(1)}, f32[2,8,480,32,4]{2,3,4,1,0:T(8,128)}) fusion(bf16[32,4,1152,1,1]{2,1,0,4,3:T(4,128)(2,1)S(1)} %bitcast.128, bf16[2,8,480,1152]{3,2,1,0:T(8,128)(2,1)S(1)} %slice_dynamic-update-slice_fusion), kind=kOutput, calls=%fused_computation.86 | convolution fusion | flops 2267873280 | bytes 21922304 | tf_op jit(solution)/shard_map/dot_general | solution.py:46
  26.8 3.9 %all-reduce.4 = (f32[2,32]{1,0:T(2,128)S(1)}, f32[2,32]{1,0:T(2,128)S(1)}) all-reduce(f32[2,32]{1,0:T(2,128)S(1)} %get-tuple-element.6, f32[2,32]{1,0:T(2,128)S(1)} %get-tuple-element.5), channel_id=1, replica_groups=mesh['tm'=16,'rows'=2] {'rows'}, use_global_device_ids=true, to_apply=%region_3.4 | all-reduce | flops 128 | bytes 1024 | tf_op jit(solution)/shard_map/psum | solution.py:53
  30.7 2.9 %subtract_multiply_fusion = f32[2,8,480,32,4]{2,3,4,1,0:T(8,128)S(1)} fusion(f32[2,8,480,32,4]{2,3,4,1,0:T(8,128)} %get-tuple-element.29, f32[2,32]{1,0:T(2,128)S(1)} %get-tuple-element.28, f32[2,32]{1,0:T(2,128)S(1)} %get-tuple-element.27), kind=kLoop, calls=%fused_computation.7 | loop fusion | flops 1966080 | bytes 7864832 | tf_op jit(solution)/shard_map/mul | solution.py:57
  33.6 0.0 copy-start.7
  33.6 0.0 copy-start.8
  33.7 2.4 %copy.15 = f32[2,8,480,32,4]{2,1,4,3,0:T(8,128)S(1)} copy(f32[2,8,480,32,4]{2,3,4,1,0:T(8,128)S(1)} %subtract_multiply_fusion) | data formatting | bytes 7864320 | tf_op jit(solution)/shard_map/mul | solution.py:57
  36.1 1.4 multiply_convert_fusion
  37.6 4.1 %slice_bitcast_fusion = (bf16[1,2,8,30,128]{3,2,4,1,0:T(8,128)(2,1)S(1)}, bf16[1,2,8,30,128]{3,2,4,1,0:T(8,128)(2,1)S(1)}, bf16[1,2,8,30,128]{3,2,4,1,0:T(8,128)...) fusion(bf16[2,8,480,128]{2,1,3,0:T(8,128)(2,1)S(1)} %multiply_c, ...), kind=kLoop, calls=%fused_computation.26 | loop fusion | bytes 3932160 | tf_op jit(solution)/shard_map/stack | solution.py:63
  41.7 1.0 copy.16
  42.7 0.9 constant_dynamic-update-slice_fusion.16
  43.6 2.1 %copy.17 = bf16[1,2,8,30,128]{4,2,3,1,0:T(8,128)(2,1)} copy(bf16[1,2,8,30,128]{3,2,4,1,0:T(8,128)(2,1)} %get-tuple-element.23) | data formatting | bytes 245760 | tf_op jit(solution)/shard_map/stack | solution.py:63
  45.6 2.1 %copy.18 = bf16[1,2,8,30,128]{4,2,3,1,0:T(8,128)(2,1)} copy(bf16[1,2,8,30,128]{3,2,4,1,0:T(8,128)(2,1)} %get-tuple-element.22) | data formatting | bytes 245760 | tf_op jit(solution)/shard_map/stack | solution.py:63
  47.7 2.1 %copy.19 = bf16[1,2,8,30,128]{4,2,3,1,0:T(8,128)(2,1)} copy(bf16[1,2,8,30,128]{3,2,4,1,0:T(8,128)(2,1)} %get-tuple-element.21) | data formatting | bytes 245760 | tf_op jit(solution)/shard_map/stack | solution.py:63
  49.8 2.1 %copy.20 = bf16[1,2,8,30,128]{4,2,3,1,0:T(8,128)(2,1)} copy(bf16[1,2,8,30,128]{3,2,4,1,0:T(8,128)(2,1)} %get-tuple-element.20) | data formatting | bytes 245760 | tf_op jit(solution)/shard_map/stack | solution.py:63
  51.8 2.1 %copy.21 = bf16[1,2,8,30,128]{4,2,3,1,0:T(8,128)(2,1)} copy(bf16[1,2,8,30,128]{3,2,4,1,0:T(8,128)(2,1)} %get-tuple-element.19) | data formatting | bytes 245760 | tf_op jit(solution)/shard_map/stack | solution.py:63
  53.9 2.1 %copy.22 = bf16[1,2,8,30,128]{4,2,3,1,0:T(8,128)(2,1)} copy(bf16[1,2,8,30,128]{3,2,4,1,0:T(8,128)(2,1)} %get-tuple-element.18) | data formatting | bytes 245760 | tf_op jit(solution)/shard_map/stack | solution.py:63
  56.0 2.1 %copy.23 = bf16[1,2,8,30,128]{4,2,3,1,0:T(8,128)(2,1)} copy(bf16[1,2,8,30,128]{3,2,4,1,0:T(8,128)(2,1)} %get-tuple-element.17) | data formatting | bytes 245760 | tf_op jit(solution)/shard_map/stack | solution.py:63
  58.0 2.0 %copy.24 = bf16[1,2,8,30,128]{4,2,3,1,0:T(8,128)(2,1)} copy(bf16[1,2,8,30,128]{3,2,4,1,0:T(8,128)(2,1)} %get-tuple-element.16) | data formatting | bytes 245760 | tf_op jit(solution)/shard_map/stack | solution.py:63
  60.1 2.1 %copy.25 = bf16[1,2,8,30,128]{4,2,3,1,0:T(8,128)(2,1)} copy(bf16[1,2,8,30,128]{3,2,4,1,0:T(8,128)(2,1)} %get-tuple-element.15) | data formatting | bytes 245760 | tf_op jit(solution)/shard_map/stack | solution.py:63
  62.1 2.1 %copy.26 = bf16[1,2,8,30,128]{4,2,3,1,0:T(8,128)(2,1)} copy(bf16[1,2,8,30,128]{3,2,4,1,0:T(8,128)(2,1)} %get-tuple-element.14) | data formatting | bytes 245760 | tf_op jit(solution)/shard_map/stack | solution.py:63
  64.2 2.1 %copy.27 = bf16[1,2,8,30,128]{4,2,3,1,0:T(8,128)(2,1)} copy(bf16[1,2,8,30,128]{3,2,4,1,0:T(8,128)(2,1)} %get-tuple-element.13) | data formatting | bytes 245760 | tf_op jit(solution)/shard_map/stack | solution.py:63
  66.3 2.1 %copy.28 = bf16[1,2,8,30,128]{4,2,3,1,0:T(8,128)(2,1)} copy(bf16[1,2,8,30,128]{3,2,4,1,0:T(8,128)(2,1)} %get-tuple-element.12) | data formatting | bytes 245760 | tf_op jit(solution)/shard_map/stack | solution.py:63
  68.3 1.0 copy.29
  69.3 0.4 copy.30
  69.7 0.4 copy.31
  70.1 0.9 constant_dynamic-update-slice_fusion.15
  71.0 0.9 constant_dynamic-update-slice_fusion.14
  72.0 0.9 constant_dynamic-update-slice_fusion.13
  72.9 0.9 constant_dynamic-update-slice_fusion.12
  73.8 0.9 constant_dynamic-update-slice_fusion.11
  74.7 0.9 constant_dynamic-update-slice_fusion.10
  75.6 0.9 constant_dynamic-update-slice_fusion.9
  76.6 0.9 constant_dynamic-update-slice_fusion.8
  77.6 0.0 copy-start.6
  77.7 54.0 %all_to_all.23 = bf16[16,2,8,30,128]{4,2,3,1,0:T(8,128)(2,1)S(1)} all-to-all(bf16[16,2,8,30,128]{4,2,3,1,0:T(8,128)(2,1)S(1)} %constant_dynamic-update-slice_fusion.1), channel_id=1, replica_groups=mesh['tm'=16,'rows'=2] {'tm'}, dimensions={0} | all-to-all | bytes 3932160 | tf_op jit(solution)/shard_map/all_to_all | solution.py:63
  131.8 0.7 fusion.22
  132.4 0.7 fusion.24
  133.1 0.9 add_convert_fusion.2
  134.0 0.6 fusion.17
  134.7 0.7 fusion.19
  135.4 1.1 add_convert_fusion.1
  136.4 0.7 fusion.12
  137.1 0.7 fusion.14
  137.8 1.0 add_convert_fusion
  138.7 49.4 %all_to_all.24 = bf16[32,8,30,128]{3,1,2,0:T(8,128)(2,1)S(1)} all-to-all(bf16[32,8,30,128]{3,1,2,0:T(8,128)(2,1)S(1)} %add_convert_fusion), channel_id=1, replica_groups=mesh['tm'=16,'rows'=2] {'tm'}, dimensions={0} | all-to-all | bytes 3932160 | tf_op jit(solution)/shard_map/all_to_all | solution.py:70
  188.1 0.1 copy.32
  188.2 1.5 copy.33
  (23 shorter events, 0.2 us)
Async XLA Ops:
  0.0 13.6 %copy-start = (bf16[2,8,480,128]{3,2,1,0:T(8,128)(2,1)S(1)}, bf16[2,8,480,128]{3,2,1,0:T(8,128)(2,1)}, u32[]{:S(2)}) copy-start(bf16[2,8,480,128]{3,2,1,0:T(8,128)(2,1)} %param.5) | copy-start | bytes 5898244
  1.2 8.6 %collective-permute-start = (bf16[2,1,480,128]{3,2,1,0:T(8,128)(2,1)S(1)}, bf16[2,1,480,128]{3,2,1,0:T(8,128)(2,1)S(1)}, u32[]{:S(2)}, u32[]{:S(2)}) collective-permute-start(bf16[2,1,480,128]{3,2,1,0:T(8,128)(2,1)S(1)} %get-tuple-element.25), channel_id=1, source_target_pairs={{0,1},{2,3},{4,5},{6,7},{8,9},{10,11},{12,13},{14,15},{16,17},{18,... | collective-permute-start | bytes 737288 | tf_op jit(solution)/shard_map/ppermute | solution.py:16
  5.2 8.4 %collective-permute-start.1 = (bf16[2,1,480,128]{3,2,1,0:T(8,128)(2,1)S(1)}, bf16[2,1,480,128]{3,2,1,0:T(8,128)(2,1)S(1)}, u32[]{:S(2)}, u32[]{:S(2)}) collective-permute-start(bf16[2,1,480,128]{3,2,1,0:T(8,128)(2,1)S(1)} %get-tuple-element.26), channel_id=1, source_target_pairs={{1,0},{3,2},{5,4},{7,6},{9,8},{11,10},{13,12},{15,14},{17,16},{19,... | collective-permute-start | bytes 737288 | tf_op jit(solution)/shard_map/ppermute | solution.py:17
  33.6 2.5 %copy-start.7 = (f32[128]{0:T(128)S(1)}, f32[128]{0:T(128)}, u32[]{:S(2)}) copy-start(f32[128]{0:T(128)} %param.8) | copy-start | bytes 1540
  33.6 2.5 %copy-start.8 = (f32[128]{0:T(128)S(1)}, f32[128]{0:T(128)}, u32[]{:S(2)}) copy-start(f32[128]{0:T(128)} %param.7) | copy-start | bytes 1540
  69.3 8.3 %copy-start.2 = (bf16[1,2,8,30,128]{4,2,3,1,0:T(8,128)(2,1)S(1)}, bf16[1,2,8,30,128]{4,2,3,1,0:T(8,128)(2,1)}, u32[]{:S(2)}) copy-start(bf16[1,2,8,30,128]{4,2,3,1,0:T(8,128)(2,1)} %copy.28) | copy-start | bytes 368644
  69.3 8.3 %copy-start.1 = (bf16[1,2,8,30,128]{4,2,3,1,0:T(8,128)(2,1)S(1)}, bf16[1,2,8,30,128]{4,2,3,1,0:T(8,128)(2,1)}, u32[]{:S(2)}) copy-start(bf16[1,2,8,30,128]{4,2,3,1,0:T(8,128)(2,1)} %copy.29) | copy-start | bytes 368644
  69.7 7.8 %copy-start.5 = (bf16[1,2,8,30,128]{4,2,3,1,0:T(8,128)(2,1)S(1)}, bf16[1,2,8,30,128]{4,2,3,1,0:T(8,128)(2,1)}, u32[]{:S(2)}) copy-start(bf16[1,2,8,30,128]{4,2,3,1,0:T(8,128)(2,1)} %copy.25) | copy-start | bytes 368644
  69.7 7.8 %copy-start.4 = (bf16[1,2,8,30,128]{4,2,3,1,0:T(8,128)(2,1)S(1)}, bf16[1,2,8,30,128]{4,2,3,1,0:T(8,128)(2,1)}, u32[]{:S(2)}) copy-start(bf16[1,2,8,30,128]{4,2,3,1,0:T(8,128)(2,1)} %copy.26) | copy-start | bytes 368644
  69.7 7.8 %copy-start.3 = (bf16[1,2,8,30,128]{4,2,3,1,0:T(8,128)(2,1)S(1)}, bf16[1,2,8,30,128]{4,2,3,1,0:T(8,128)(2,1)}, u32[]{:S(2)}) copy-start(bf16[1,2,8,30,128]{4,2,3,1,0:T(8,128)(2,1)} %copy.27) | copy-start | bytes 368644
  77.6 54.1 %copy-start.6 = (bf16[3,3,128,128]{3,2,1,0:T(8,128)(2,1)S(1)}, bf16[3,3,128,128]{3,2,1,0:T(8,128)(2,1)}, u32[]{:S(2)}) copy-start(bf16[3,3,128,128]{3,2,1,0:T(8,128)(2,1)} %param.9) | copy-start | bytes 884740
